TPU v7x, 256 devices: a whole 4x4x8 slice. The times are simulated.
256 devices in a mesh: row: 32 (over z_lo, y, x), col: 8 (over z_hi, core).
Axes of the slice: x: 4, y: 4, z: 8 (z_hi: 4, z_lo: 2; z = z_hi * 2 + z_lo), core: 2. Of those that a mesh axis runs over, the one named last changes fastest.
Arguments:
- c_left: float32 [32, 8, 2048, 256], P('row', 'col'), may hold values from -6 to 6
- c_right: float32 [32, 8, 2048, 256], P('row', 'col'), may hold values from -6 to 6
- c_rank: int32 [32, 8], P('row', 'col'), may hold values from 32 to 256, as said below
- a_left: bfloat16 [32, 2, 2048, 256], P('row', None, 'col'), may hold values from -6 to 6
- a_right: bfloat16 [32, 2, 2048, 256], P('row', None, 'col'), may hold values from -0.125 to 0.125
- a_rank: int32 [32, 2], P('row'), may hold values from 32 to 256, as said below
- a_pattern: int32 [32, 2], P('row'), may hold values 0 or 1
- b_left: bfloat16 [2, 8, 2048, 256], P(None, 'col', 'row'), may hold values from -6 to 6
- b_right: bfloat16 [2, 8, 2048, 256], P(None, 'col', 'row'), may hold values from -0.375 to 0.375
- b_rank: int32 [2, 8], P(None, 'col'), may hold values from 32 to 256, as said below
- b_pattern: int32 [2, 8], P(None, 'col'), may hold values 0 or 1
- probe: bfloat16 [2, 2048, 256], replicated, may hold values from -6 to 6
- target: int32 [32, 8, 2], P('row', 'col'), may hold values from 16 to 240, as said below
Outputs:
- out_left: float32 [32, 8, 2048, 256], P('row', 'col')
- out_right: float32 [32, 8, 2048, 256], P('row', 'col')
Inputs may be any that keep to these rules, and one draw needn't show every extreme that they name: `c_rank`: every rank lies from 32 to 256; both ends are taken by some tile. `a_rank`: every rank lies from 32 to 256; both ends are taken by some tile. `b_rank`: every rank lies from 32 to 256; both ends are taken by some tile. With g(r) = max(8, r // 16): target[i, j, 0] <= c_rank[i, j] - g(c_rank[i, j]) and target[i, j, k] <= target[i, j, k - 1] - g(target[i, j, k - 1]); both ends are taken by some tile.
All inputs are finite; a program needn't handle non-finite values. No bound on the sum of `a_pattern` or of `b_pattern` on one device may be relied on, other than what follows from the above.
Results may differ from a plain program's by a relative error of at most 0.0009.
Values may be sent and summed in bfloat16 or wider, within the bound.
A program may use at most 128 MiB of HBM per device.

v0:
```python
import math
import jax
import jax.numpy as jnp
from jax import lax
from jax.sharding import PartitionSpec as P


def column_mask(count, width):
    return (jnp.arange(width, dtype=jnp.int32) < count).astype(jnp.float32)


def product_of(left, right):
    return jnp.dot(left, right, precision=lax.Precision.HIGHEST, preferred_element_type=jnp.float32)


def transposed_product(left, right):
    return lax.dot_general(
        left,
        right,
        (((0,), (0,)), ((), ())),
        precision=lax.Precision.HIGHEST,
        preferred_element_type=jnp.float32,
    )


def recompress(left, right, keep, extra, extra_right, right_probe, probe_step, tmask):
    tile = left.shape[0]
    probe_cols = probe_step.astype(jnp.float32) * tmask[None, :]
    core_c = transposed_product(right, probe_cols) * keep[:, None]
    core_b = right_probe * tmask[None, :]
    sample = product_of(left, core_c) + product_of(extra, core_b)
    gram = transposed_product(sample, sample) + jnp.diag(1.0 - tmask)
    factor = jnp.linalg.cholesky(gram)
    basis = lax.linalg.triangular_solve(
        factor, sample, left_side=False, lower=True, transpose_a=True
    )
    back_c = transposed_product(left, basis) * keep[:, None]
    back_b = transposed_product(extra, basis)
    new_right = (product_of(right, back_c) + product_of(extra_right, back_b)) / math.sqrt(tile)
    return (basis * math.sqrt(tile), new_right)


def on_device(
    c_left,
    c_right,
    c_rank,
    a_left,
    a_right,
    a_rank,
    a_pattern,
    b_left,
    b_right,
    b_rank,
    b_pattern,
    probe,
    target,
):
    width = c_left.shape[3]
    steps = probe.shape[0]
    left = c_left[0, 0]
    right = c_right[0, 0]
    keep = column_mask(c_rank[0, 0], width)
    for step in range(steps):
        a_l, a_r = (
            lax.all_gather(a_left[0, step], "col", axis=0, tiled=True),
            lax.all_gather(a_right[0, step], "col", axis=0, tiled=True),
        )
        b_r = lax.all_gather(b_right[step, 0], "row", axis=0, tiled=True)

        def add_middle(total, piece, start, a_rows=a_r):
            return lax.dot_general(
                a_rows, piece, (((0,), (0,)), ((), ())), preferred_element_type=jnp.float32
            )

        middle = add_middle(
            jnp.zeros((width, width), jnp.float32),
            lax.all_gather(b_left[step, 0], "row", axis=0, tiled=True),
            jnp.int32(0),
        )
        weight = (a_pattern[0, step] * b_pattern[step, 0]).astype(jnp.float32)
        middle = (
            middle
            * column_mask(a_rank[0, step], width)[:, None]
            * column_mask(b_rank[step, 0], width)[None, :]
            * weight
        )
        extra = product_of(a_l.astype(jnp.float32), middle)
        right_probe = lax.dot_general(
            b_r, probe[step], (((0,), (0,)), ((), ())), preferred_element_type=jnp.float32
        )
        tmask = column_mask(target[0, 0, step], width)
        left, right = recompress(
            left, right, keep, extra, b_r.astype(jnp.float32), right_probe, probe[step], tmask
        )
        keep = tmask
    return (left[None, None], right[None, None])


def solution(mesh):
    return jax.shard_map(
        on_device,
        mesh=mesh,
        in_specs=(
            P("row", "col", None, None),
            P("row", "col", None, None),
            P("row", "col"),
            P("row", None, "col", None),
            P("row", None, "col", None),
            P("row", None),
            P("row", None),
            P(None, "col", "row", None),
            P(None, "col", "row", None),
            P(None, "col"),
            P(None, "col"),
            P(),
            P("row", "col", None),
        ),
        out_specs=(P("row", "col", None, None), P("row", "col", None, None)),
        check_vma=False,
    )
```

profile of v0, /device:TPU:1, one launch (start us, length us, event | category | flops | bytes accessed | tf_op | source)
XLA Modules:
  0.0 865.4 jit_solution(7371660439607618762)
XLA Ops:
  31.7 5.4 fusion.23
  37.1 3.3 convolution_bitcast_fusion.1
  40.4 104.2 %all-gather.23.cloned.1.call-done = bf16[1,1,2048,256]{3,2,1,0:T(8,128)(2,1)} async-done(((bf16[1,1,64,256]{3,2,1,0:T(8,128)(2,1)}), bf16[1,1,2048,256]{3,2,1,0:T(8,128)(2,1)}) %all-gather.23.cloned.1.call-update) | async-done | bytes 1048592 | tf_op jit(solution)/shard_map/all_gather | solution.py:68
  146.6 53.8 %all-gather.17.cloned.1.call-done = bf16[1,1,2048,256]{3,2,1,0:T(8,128)(2,1)} async-done(((bf16[1,1,256,256]{3,2,1,0:T(8,128)(2,1)}), bf16[1,1,2048,256]{3,2,1,0:T(8,128)(2,1)}) %all-gather.17.cloned.1.call-update) | async-done | bytes 1048592 | tf_op jit(solution)/shard_map/all_gather | solution.py:66
  200.4 130.3 %all-gather.19.cloned.1.call-done = bf16[1,1,2048,256]{3,2,1,0:T(8,128)(2,1)} async-done(((bf16[1,1,64,256]{3,2,1,0:T(8,128)(2,1)}), bf16[1,1,2048,256]{3,2,1,0:T(8,128)(2,1)}) %all-gather.19.cloned.1.call-update) | async-done | bytes 1048592 | tf_op jit(solution)/shard_map/all_gather | solution.py:77
  332.7 53.1 %all-gather.21.cloned.1.call-done = bf16[1,1,2048,256]{3,2,1,0:T(8,128)(2,1)} async-done(((bf16[1,1,256,256]{3,2,1,0:T(8,128)(2,1)}), bf16[1,1,2048,256]{3,2,1,0:T(8,128)(2,1)}) %all-gather.21.cloned.1.call-update) | async-done | bytes 1048592 | tf_op jit(solution)/shard_map/all_gather | solution.py:65
  385.8 3.2 fusion.54
  394.8 11.7 %cholesky.130 = f32[128,128]{1,0:T(8,128)S(1)} custom-call(f32[128,128]{1,0:T(8,128)S(1)} %cholesky.194), custom_call_target="Cholesky" | custom-call | tf_op jit(solution)/shard_map/jit(cholesky)/cholesky | solution.py:33
  407.2 9.8 %custom-call.13 = f32[1,128,128]{1,2,0:T(8,128)S(1)} custom-call(f32[1,128,128]{2,1,0:T(8,128)S(1)} %get-tuple-element.57), custom_call_target="InvertDiagBlocksLowerTriangular" | custom-call | tf_op jit(solution)/shard_map/jit(cholesky)/cholesky | solution.py:33
  417.5 11.7 %cholesky.147 = f32[128,128]{1,0:T(8,128)S(1)} custom-call(f32[128,128]{1,0:T(8,128)S(1)} %convolution_subtract_fusion.3), custom_call_target="Cholesky" | custom-call | tf_op jit(solution)/shard_map/jit(cholesky)/cholesky | solution.py:33
  431.3 4.0 while.4
  435.9 20.1 %custom-call.14 = f32[2,128,128]{1,2,0:T(8,128)S(1)} custom-call(f32[2,128,128]{2,1,0:T(8,128)S(1)} %get-tuple-element.18), custom_call_target="InvertDiagBlocksLowerTriangular" | custom-call | tf_op jit(solution)/shard_map/triangular_solve/custom-call.0 | solution.py:34
  456.0 2.4 fusion.40
  469.8 2.2 fusion.20
  472.1 4.8 fusion.17
  476.8 39.2 %all-gather.31.cloned.1.call-done = bf16[1,1,2048,256]{3,2,1,0:T(8,128)(2,1)} async-done(((bf16[1,1,64,256]{3,2,1,0:T(8,128)(2,1)}), bf16[1,1,2048,256]{3,2,1,0:T(8,128)(2,1)}) %all-gather.31.cloned.1.call-update) | async-done | bytes 1048592 | tf_op jit(solution)/shard_map/all_gather | solution.py:68
  518.1 54.1 %all-gather.25.cloned.1.call-done = bf16[1,1,2048,256]{3,2,1,0:T(8,128)(2,1)} async-done(((bf16[1,1,256,256]{3,2,1,0:T(8,128)(2,1)}), bf16[1,1,2048,256]{3,2,1,0:T(8,128)(2,1)}) %all-gather.25.cloned.1.call-update) | async-done | bytes 1048592 | tf_op jit(solution)/shard_map/all_gather | solution.py:66
  572.2 130.3 %all-gather.27.cloned.1.call-done = bf16[1,1,2048,256]{3,2,1,0:T(8,128)(2,1)} async-done(((bf16[1,1,64,256]{3,2,1,0:T(8,128)(2,1)}), bf16[1,1,2048,256]{3,2,1,0:T(8,128)(2,1)}) %all-gather.27.cloned.1.call-update) | async-done | bytes 1048592 | tf_op jit(solution)/shard_map/all_gather | solution.py:77
  702.5 2.7 fusion.35
  705.2 52.5 %all-gather.29.cloned.1.call-done = bf16[1,1,2048,256]{3,2,1,0:T(8,128)(2,1)} async-done(((bf16[1,1,256,256]{3,2,1,0:T(8,128)(2,1)}), bf16[1,1,2048,256]{3,2,1,0:T(8,128)(2,1)}) %all-gather.29.cloned.1.call-update) | async-done | bytes 1048592 | tf_op jit(solution)/shard_map/all_gather | solution.py:65
  757.7 3.3 fusion.44
  761.1 3.6 convolution_add_fusion.1
  766.0 3.8 convolution_add_fusion.4
  772.4 11.7 %cholesky.164 = f32[128,128]{1,0:T(8,128)S(1)} custom-call(f32[128,128]{1,0:T(8,128)S(1)} %cholesky.197), custom_call_target="Cholesky" | custom-call | tf_op jit(solution)/shard_map/jit(cholesky)/cholesky | solution.py:33
  784.8 9.8 %custom-call.15 = f32[1,128,128]{1,2,0:T(8,128)S(1)} custom-call(f32[1,128,128]{2,1,0:T(8,128)S(1)} %get-tuple-element.49), custom_call_target="InvertDiagBlocksLowerTriangular" | custom-call | tf_op jit(solution)/shard_map/jit(cholesky)/cholesky | solution.py:33
  796.8 12.1 %cholesky.181 = f32[128,128]{1,0:T(8,128)S(1)} custom-call(f32[128,128]{1,0:T(8,128)S(1)} %convolution_subtract_fusion.2), custom_call_target="Cholesky" | custom-call | tf_op jit(solution)/shard_map/jit(cholesky)/cholesky | solution.py:33
  812.0 4.0 while.5
  816.7 20.5 %custom-call.16 = f32[2,128,128]{1,2,0:T(8,128)S(1)} custom-call(f32[2,128,128]{2,1,0:T(8,128)} %copy-done.22), custom_call_target="InvertDiagBlocksLowerTriangular" | custom-call | tf_op jit(solution)/shard_map/triangular_solve/custom-call.0 | solution.py:34
  837.2 2.4 fusion.38
  842.6 2.7 fusion.28
  848.6 3.1 copy.23
  853.4 5.0 fusion.1
  (142 shorter events, 71.8 us)
Async XLA Ops:
  7.2 30.0 %copy-start = (f32[1,1,2048,256]{3,2,1,0:T(8,128)S(1)}, f32[1,1,2048,256]{3,2,1,0:T(8,128)}, u32[]{:S(2)}) copy-start(f32[1,1,2048,256]{3,2,1,0:T(8,128)} %param.16) | copy-start | bytes 6291460
  7.2 137.4 %all-gather.23.cloned.1.call-start = ((), (), s32[]{:S(2)}) async-start(), calls=%async_computation.3 | async-start | bytes 1081344 | tf_op jit(solution)/shard_map/all_gather | solution.py:68
  8.8 191.6 %all-gather.17.cloned.1.call-start = ((), (), s32[]{:S(2)}) async-start(), calls=%async_computation | async-start | bytes 1179648 | tf_op jit(solution)/shard_map/all_gather | solution.py:66
  10.5 320.1 %all-gather.19.cloned.1.call-start = ((), (), s32[]{:S(2)}) async-start(), calls=%async_computation.1 | async-start | bytes 1081344 | tf_op jit(solution)/shard_map/all_gather | solution.py:77
  12.0 373.8 %all-gather.21.cloned.1.call-start = ((), (), s32[]{:S(2)}) async-start(), calls=%async_computation.2 | async-start | bytes 1179648 | tf_op jit(solution)/shard_map/all_gather | solution.py:65
  13.8 502.3 %all-gather.31.cloned.1.call-start = ((), (), s32[]{:S(2)}) async-start(), calls=%async_computation.7 | async-start | bytes 1081344 | tf_op jit(solution)/shard_map/all_gather | solution.py:68
  14.4 557.8 %all-gather.25.cloned.1.call-start = ((), (), s32[]{:S(2)}) async-start(), calls=%async_computation.4 | async-start | bytes 1179648 | tf_op jit(solution)/shard_map/all_gather | solution.py:66
  14.9 687.5 %all-gather.27.cloned.1.call-start = ((), (), s32[]{:S(2)}) async-start(), calls=%async_computation.5 | async-start | bytes 1081344 | tf_op jit(solution)/shard_map/all_gather | solution.py:77
  15.7 742.0 %all-gather.29.cloned.1.call-start = ((), (), s32[]{:S(2)}) async-start(), calls=%async_computation.6 | async-start | bytes 1179648 | tf_op jit(solution)/shard_map/all_gather | solution.py:65
  21.4 19.0 %copy-start.23 = (f32[256]{0:T(256)}, f32[256]{0:T(256)S(1)}, u32[]{:S(2)}) copy-start(f32[256]{0:T(256)S(1)} %compare_convert_fusion.5) | copy-start | bytes 3076
  385.8 3.3 copy-start.15
  389.1 2.1 copy-start.9
  391.2 1.3 copy-start.3
  456.0 2.4 copy-start.4
  458.4 2.2 copy-start.10
  460.6 11.4 %copy-start.11 = (f32[2048,128]{0,1:T(8,128)}, f32[2048,128]{0,1:T(8,128)S(1)}, u32[]{:S(2)}) copy-start(f32[2048,128]{0,1:T(8,128)S(1)} %fusion.73) | copy-start | bytes 3145732
  460.6 1.9 copy-start.18
  462.6 1.9 copy-start.24
  464.4 1.9 copy-start.13
  466.4 3.5 copy-start.16
  468.5 1.3 copy-start.5
  757.7 3.3 copy-start.14
  761.1 3.6 copy-start.7
  761.1 4.9 copy-start.25
  769.8 42.2 %copy-start.27 = (s32[2,2]{1,0:T(2,128)S(1)}, s32[2,2]{1,0:T(2,128)}, u32[]{:S(2)}) copy-start(s32[2,2]{1,0:T(2,128)} %copy-done.26) | copy-start | bytes 52
  808.9 2.1 copy-start.19
  837.2 2.5 copy-start.2
  839.6 2.9 copy-start.12
  842.6 2.7 copy-start.8
  848.6 3.1 copy-start.17
  851.8 1.6 copy-start.6
  851.8 1.6 copy-start.21
  (4 other events, 3.2 us)
Sparse Core Ops, SparseCore 0:
  9.8 134.7 all-gather.22
  147.0 53.3 all-gather.16
  202.2 128.4 all-gather.18
  332.4 53.3 all-gather.20
  387.4 128.5 all-gather.30
  517.8 54.3 all-gather.24
  574.0 128.4 all-gather.26
  704.3 53.3 all-gather.28
where the time goes:
time: 875 us; the launch traced here: 865 us
  waiting for transfers between devices  620 us (71%)
  other arithmetic  119 us (14%)
  matrix products  73.3 us (8%)
  local copies, waits for them, and re-layouts  31.6 us (4%)
  between operations  20.7 us (2%)
    all_gather x2, waiting for transfers between devices, on_device(): lax.all_gather(b_left[step, 0], 'row', axis=0, tiled=True)  261 us
    all_gather x2, waiting for transfers between devices, on_device(): b_r = lax.all_gather(b_right[step, 0], 'row', axis=0, tiled=True)  143 us
    all_gather x2, waiting for transfers between devices, on_device(): lax.all_gather(a_right[0, step], 'col', axis=0, tiled=True)  108 us
    all_gather x2, waiting for transfers between devices, on_device(): lax.all_gather(a_left[0, step], 'col', axis=0, tiled=True)  106 us
    another operation x14, other arithmetic, recompress(): factor = jnp.linalg.cholesky(gram)  69.7 us
    another operation x5, other arithmetic, recompress(): lax.linalg.triangular_solve(factor, sample, left_side=False, lower=True,...  41.6 us
    dot_general x10, matrix products, product_of(): jnp.dot(left, right, precision=lax.Precision.HIGHEST, preferred_element_t...  30.3 us
    dot_general x8, matrix products, transposed_product(): lax.dot_general(left, right, (((0,), (0,)), ((), ())), precision=lax.Prec...  21.8 us
  transfers between devices with their start and end apart: 8, of which 8 were waited for; matrix products, arithmetic and copies ran while one was open for 14% of the time, Pallas kernels for 0%

commit v1 on v0

--- a/solution.py
+++ b/solution.py
@@ -65,7 +65,21 @@
             lax.all_gather(a_left[0, step], "col", axis=0, tiled=True),
             lax.all_gather(a_right[0, step], "col", axis=0, tiled=True),
         )
-        b_r = lax.all_gather(b_right[step, 0], "row", axis=0, tiled=True)
+
+        def press_run(local_values, lane_axis):
+            return jnp.concatenate(
+                lax.all_to_all(
+                    jnp.stack(
+                        tuple((local_values for _ in range(lax.axis_size(lane_axis)))), axis=0
+                    ),
+                    axis_name=lane_axis,
+                    split_axis=0,
+                    concat_axis=0,
+                ),
+                axis=0,
+            )
+
+        b_r = press_run(b_right[step, 0], "row")
 
         def add_middle(total, piece, start, a_rows=a_r):
             return lax.dot_general(

time: 875 us -> 563 us (0.64)
  waiting for transfers between devices: 620 us -> 299 us
  starting transfers between devices: 0.32 us -> 15.5 us
    all_gather x2 -> x0, waiting for transfers between devices: 143 us -> none  [on_device(): b_r = lax.all_gather(b_right[step, 0], 'row', axis=0, tiled=True)]
    all_gather x2, waiting for transfers between devices: 108 us -> 0.04 us  [on_device(): lax.all_gather(a_right[0, step], 'col', axis=0, tiled=True)]
    all_gather x2, waiting for transfers between devices: 261 us -> 190 us  [on_device(): lax.all_gather(b_left[step, 0], 'row', axis=0, tiled=True)]
    all_to_all x0 -> x2, starting transfers between devices: none -> 15.2 us  [press_run(): lax.all_to_all(jnp.stack(tuple((local_values for _ in range(lax.axis_size...]
  transfers between devices with their start and end apart: 8 -> 8, of which waited for: 8 -> 5; matrix products, arithmetic and copies ran while one was open for 14% -> 21% of each run, Pallas kernels for 0% -> 0%
where the time goes in v1:
time: 563 us; the launch traced here: 557 us
  waiting for transfers between devices  299 us (53%)
  other arithmetic  119 us (21%)
  matrix products  73.7 us (13%)
  local copies, waits for them, and re-layouts  29.1 us (5%)
  between operations  20.8 us (4%)
  starting transfers between devices  15.5 us (3%)
    all_gather x2, waiting for transfers between devices, on_device(): lax.all_gather(b_left[step, 0], 'row', axis=0, tiled=True)  190 us
    all_gather x2, waiting for transfers between devices, on_device(): lax.all_gather(a_left[0, step], 'col', axis=0, tiled=True)  105 us
    another operation x14, other arithmetic, recompress(): factor = jnp.linalg.cholesky(gram)  69.7 us
    another operation x5, other arithmetic, recompress(): lax.linalg.triangular_solve(factor, sample, left_side=False, lower=True,...  41.4 us
    dot_general x10, matrix products, product_of(): jnp.dot(left, right, precision=lax.Precision.HIGHEST, preferred_element_t...  31.6 us
    dot_general x8, matrix products, transposed_product(): lax.dot_general(left, right, (((0,), (0,)), ((), ())), precision=lax.Prec...  21.1 us
    all_to_all x2, starting transfers between devices, press_run(): lax.all_to_all(jnp.stack(tuple((local_values for _ in range(lax.axis_size...  15.2 us
  transfers between devices with their start and end apart: 8, of which 5 were waited for; matrix products, arithmetic and copies ran while one was open for 21% of the time, Pallas kernels for 0%

profile of v1, /device:TPU:1, one launch (start us, length us, event | category | flops | bytes accessed | tf_op | source)
XLA Modules:
  0.0 556.7 jit_solution(13705161608626912432)
XLA Ops:
  15.4 9.2 %all-to-all-start = ((bf16[32,64,256]{2,1,0:T(8,128)(2,1)}), bf16[32,64,256]{2,1,0:T(8,128)(2,1)S(1)}, u32[]{:S(2)}, u32[]{:S(2)}) async-start(bf16[32,64,256]{2,1,0:T(8,128)(2,1)} %stack.6), calls=%async_computation | async-start | bytes 2097152 | tf_op jit(solution)/shard_map/all_to_all | solution.py:71
  36.8 5.4 fusion.23
  42.2 3.3 convolution_bitcast_fusion.1
  45.5 2.4 all-to-all-done
  49.2 6.0 %all-to-all-start.1 = ((bf16[32,64,256]{2,1,0:T(8,128)(2,1)}), bf16[32,64,256]{2,1,0:T(8,128)(2,1)}, u32[]{:S(2)}, u32[]{:S(2)}) async-start(bf16[32,64,256]{2,1,0:T(8,128)(2,1)} %stack.7), calls=%async_computation.1 | async-start | bytes 2097152 | tf_op jit(solution)/shard_map/all_to_all | solution.py:71
  56.9 121.8 %all-gather.15.cloned.1.call-done = bf16[1,1,2048,256]{3,2,1,0:T(8,128)(2,1)} async-done(((bf16[1,1,64,256]{3,2,1,0:T(8,128)(2,1)}), bf16[1,1,2048,256]{3,2,1,0:T(8,128)(2,1)}) %all-gather.15.cloned.1.call-update) | async-done | bytes 1048592 | tf_op jit(solution)/shard_map/all_gather | solution.py:91
  180.8 52.5 %all-gather.17.cloned.1.call-done = bf16[1,1,2048,256]{3,2,1,0:T(8,128)(2,1)} async-done(((bf16[1,1,256,256]{3,2,1,0:T(8,128)(2,1)}), bf16[1,1,2048,256]{3,2,1,0:T(8,128)(2,1)}) %all-gather.17.cloned.1.call-update) | async-done | bytes 1048592 | tf_op jit(solution)/shard_map/all_gather | solution.py:65
  233.3 3.2 fusion.49
  242.1 11.7 %cholesky.130 = f32[128,128]{1,0:T(8,128)S(1)} custom-call(f32[128,128]{1,0:T(8,128)S(1)} %cholesky.194), custom_call_target="Cholesky" | custom-call | tf_op jit(solution)/shard_map/jit(cholesky)/cholesky | solution.py:33
  254.5 9.9 %custom-call.13 = f32[1,128,128]{1,2,0:T(8,128)S(1)} custom-call(f32[1,128,128]{2,1,0:T(8,128)S(1)} %get-tuple-element.57), custom_call_target="InvertDiagBlocksLowerTriangular" | custom-call | tf_op jit(solution)/shard_map/jit(cholesky)/cholesky | solution.py:33
  265.0 11.7 %cholesky.147 = f32[128,128]{1,0:T(8,128)S(1)} custom-call(f32[128,128]{1,0:T(8,128)S(1)} %convolution_subtract_fusion.3), custom_call_target="Cholesky" | custom-call | tf_op jit(solution)/shard_map/jit(cholesky)/cholesky | solution.py:33
  278.9 4.2 while.4
  283.7 19.9 %custom-call.14 = f32[2,128,128]{1,2,0:T(8,128)S(1)} custom-call(f32[2,128,128]{2,1,0:T(8,128)S(1)} %get-tuple-element.18), custom_call_target="InvertDiagBlocksLowerTriangular" | custom-call | tf_op jit(solution)/shard_map/triangular_solve/custom-call.0 | solution.py:34
  303.5 2.4 fusion.40
  313.9 2.1 fusion.2
  317.4 2.4 fusion.20
  319.8 4.8 fusion.17
  326.7 67.7 %all-gather.21.cloned.1.call-done = bf16[1,1,2048,256]{3,2,1,0:T(8,128)(2,1)} async-done(((bf16[1,1,64,256]{3,2,1,0:T(8,128)(2,1)}), bf16[1,1,2048,256]{3,2,1,0:T(8,128)(2,1)}) %all-gather.21.cloned.1.call-update) | async-done | bytes 1048592 | tf_op jit(solution)/shard_map/all_gather | solution.py:91
  394.4 2.7 fusion.35
  397.1 52.4 %all-gather.23.cloned.1.call-done = bf16[1,1,2048,256]{3,2,1,0:T(8,128)(2,1)} async-done(((bf16[1,1,256,256]{3,2,1,0:T(8,128)(2,1)}), bf16[1,1,2048,256]{3,2,1,0:T(8,128)(2,1)}) %all-gather.23.cloned.1.call-update) | async-done | bytes 1048592 | tf_op jit(solution)/shard_map/all_gather | solution.py:65
  449.5 3.3 fusion.42
  452.8 3.6 convolution_add_fusion.1
  457.7 3.8 convolution_add_fusion.4
  464.1 11.7 %cholesky.164 = f32[128,128]{1,0:T(8,128)S(1)} custom-call(f32[128,128]{1,0:T(8,128)S(1)} %cholesky.197), custom_call_target="Cholesky" | custom-call | tf_op jit(solution)/shard_map/jit(cholesky)/cholesky | solution.py:33
  476.5 9.8 %custom-call.15 = f32[1,128,128]{1,2,0:T(8,128)S(1)} custom-call(f32[1,128,128]{2,1,0:T(8,128)S(1)} %get-tuple-element.49), custom_call_target="InvertDiagBlocksLowerTriangular" | custom-call | tf_op jit(solution)/shard_map/jit(cholesky)/cholesky | solution.py:33
  488.5 11.7 %cholesky.181 = f32[128,128]{1,0:T(8,128)S(1)} custom-call(f32[128,128]{1,0:T(8,128)S(1)} %convolution_subtract_fusion.2), custom_call_target="Cholesky" | custom-call | tf_op jit(solution)/shard_map/jit(cholesky)/cholesky | solution.py:33
  503.3 3.8 while.5
  507.8 20.5 %custom-call.16 = f32[2,128,128]{1,2,0:T(8,128)S(1)} custom-call(f32[2,128,128]{2,1,0:T(8,128)} %copy-done.21), custom_call_target="InvertDiagBlocksLowerTriangular" | custom-call | tf_op jit(solution)/shard_map/triangular_solve/custom-call.0 | solution.py:34
  528.3 2.4 fusion.38
  539.0 3.1 copy.23
  542.1 2.4 convolution_bitcast_fusion
  544.6 5.0 fusion.1
  (150 shorter events, 66.7 us)
Async XLA Ops:
  7.2 35.0 %copy-start = (f32[1,1,2048,256]{3,2,1,0:T(8,128)S(1)}, f32[1,1,2048,256]{3,2,1,0:T(8,128)}, u32[]{:S(2)}) copy-start(f32[1,1,2048,256]{3,2,1,0:T(8,128)} %param.16) | copy-start | bytes 6291460
  7.2 49.7 %all-gather.13.cloned.1.call-start = ((), (), s32[]{:S(2)}) async-start(), calls=%async_computation.2 | async-start | bytes 1179648 | tf_op jit(solution)/shard_map/all_gather | solution.py:66
  9.1 169.7 %all-gather.15.cloned.1.call-start = ((), (), s32[]{:S(2)}) async-start(), calls=%async_computation.3 | async-start | bytes 1081344 | tf_op jit(solution)/shard_map/all_gather | solution.py:91
  10.5 14.7 %copy-start.24 = (s32[1,2]{1,0:T(1,128)S(1)}, s32[1,2]{1,0:T(1,128)}, u32[]{:S(2)}) copy-start(s32[1,2]{1,0:T(1,128)} %param.22) | copy-start | bytes 28
  10.6 15.9 %copy-start.25 = (s32[2,1]{0,1:T(1,128)S(1)}, s32[2,1]{0,1:T(1,128)}, u32[]{:S(2)}) copy-start(s32[2,1]{0,1:T(1,128)} %param.26) | copy-start | bytes 28
  10.6 19.0 %copy-start.26 = (s32[1,1,2]{2,1,0:T(1,128)S(1)}, s32[1,1,2]{2,1,0:T(1,128)}, u32[]{:S(2)}) copy-start(s32[1,1,2]{2,1,0:T(1,128)} %param.28) | copy-start | bytes 28
  10.6 22.6 %copy-start.27 = (s32[1,2]{1,0:T(1,128)S(1)}, s32[1,2]{1,0:T(1,128)}, u32[]{:S(2)}) copy-start(s32[1,2]{1,0:T(1,128)} %param.21) | copy-start | bytes 28
  10.6 23.2 %copy-start.28 = (s32[2,1]{0,1:T(1,128)S(1)}, s32[2,1]{0,1:T(1,128)}, u32[]{:S(2)}) copy-start(s32[2,1]{0,1:T(1,128)} %param.25) | copy-start | bytes 28
  10.6 222.7 %all-gather.17.cloned.1.call-start = ((), (), s32[]{:S(2)}) async-start(), calls=%async_computation.4 | async-start | bytes 1179648 | tf_op jit(solution)/shard_map/all_gather | solution.py:65
  12.4 314.3 %all-gather.19.cloned.1.call-start = ((), (), s32[]{:S(2)}) async-start(), calls=%async_computation.5 | async-start | bytes 1179648 | tf_op jit(solution)/shard_map/all_gather | solution.py:66
  12.9 381.4 %all-gather.21.cloned.1.call-start = ((), (), s32[]{:S(2)}) async-start(), calls=%async_computation.6 | async-start | bytes 1081344 | tf_op jit(solution)/shard_map/all_gather | solution.py:91
  15.4 32.5 %all-to-all-start = ((bf16[32,64,256]{2,1,0:T(8,128)(2,1)}), bf16[32,64,256]{2,1,0:T(8,128)(2,1)S(1)}, u32[]{:S(2)}, u32[]{:S(2)}) async-start(bf16[32,64,256]{2,1,0:T(8,128)(2,1)} %stack.6), calls=%async_computation | async-start | bytes 2097152 | tf_op jit(solution)/shard_map/all_to_all | solution.py:71
  24.6 424.8 %all-gather.23.cloned.1.call-start = ((), (), s32[]{:S(2)}) async-start(), calls=%async_computation.7 | async-start | bytes 1179648 | tf_op jit(solution)/shard_map/all_gather | solution.py:65
  33.2 12.3 %copy-start.22 = (f32[256]{0:T(256)}, f32[256]{0:T(256)S(1)}, u32[]{:S(2)}) copy-start(f32[256]{0:T(256)S(1)} %compare_convert_fusion.5) | copy-start | bytes 3076
  47.9 9.0 %copy-start.13 = (bf16[32,64,256]{2,1,0:T(8,128)(2,1)}, bf16[32,64,256]{2,1,0:T(8,128)(2,1)S(1)}, u32[]{:S(2)}) copy-start(bf16[32,64,256]{2,1,0:T(8,128)(2,1)S(1)} %all-to-all-done) | copy-start | bytes 3145732
  49.2 275.5 %all-to-all-start.1 = ((bf16[32,64,256]{2,1,0:T(8,128)(2,1)}), bf16[32,64,256]{2,1,0:T(8,128)(2,1)}, u32[]{:S(2)}, u32[]{:S(2)}) async-start(bf16[32,64,256]{2,1,0:T(8,128)(2,1)} %stack.7), calls=%async_computation.1 | async-start | bytes 2097152 | tf_op jit(solution)/shard_map/all_to_all | solution.py:71
  233.3 3.3 copy-start.16
  236.6 2.1 copy-start.9
  303.5 2.4 copy-start.4
  306.0 2.2 copy-start.10
  308.1 11.7 %copy-start.11 = (f32[2048,128]{0,1:T(8,128)}, f32[2048,128]{0,1:T(8,128)S(1)}, u32[]{:S(2)}) copy-start(f32[2048,128]{0,1:T(8,128)S(1)} %fusion.68) | copy-start | bytes 3145732
  308.2 1.9 copy-start.14
  312.0 1.9 copy-start.15
  313.9 3.5 copy-start.18
  449.5 3.3 copy-start.17
  452.8 3.6 copy-start.7
  452.8 4.9 copy-start.29
  461.5 41.8 %copy-start.31 = (s32[2,2]{1,0:T(2,128)S(1)}, s32[2,2]{1,0:T(2,128)}, u32[]{:S(2)}) copy-start(s32[2,2]{1,0:T(2,128)} %copy-done.30) | copy-start | bytes 52
  528.2 2.5 copy-start.2
  530.7 2.9 copy-start.12
  533.7 2.0 copy-start.8
  542.1 2.4 copy-start.6
  (8 other events, 9.6 us)
Sparse Core Ops, SparseCore 0:
  9.8 36.1 all-gather.12
  47.9 130.8 all-gather.14
  180.6 52.6 all-gather.16
  235.0 27.9 all-gather.18
  264.7 129.6 all-gather.20
  396.1 53.3 all-gather.22
